TPU v7x, 1024 devices: a whole 4x8x16 slice. The times are simulated.
1024 devices in a mesh: replica: 64 (over z_hi, y, x), tensor: 16 (over z_lo, core).
Axes of the slice: x: 4, y: 8, z: 16 (z_hi: 2, z_lo: 8; z = z_hi * 8 + z_lo), core: 2. Of those that a mesh axis runs over, the one named last changes fastest.
Arguments:
- train_hidden: bfloat16 [1024, 14784], P(None, 'replica'), may hold values from -6 to 6
- out_grad: bfloat16 [1024, 4096], P('tensor'), may hold values from -6 to 6
- master: float32 [14784, 4096], P('replica', 'tensor'), may hold values from -0.046875 to 0.046875
- first_moment: float32 [14784, 4096], P('replica', 'tensor'), may hold values from -6 to 6
- second_moment: float32 [14784, 4096], P('replica', 'tensor'), may hold values from 0.25 to 4
- decode_hidden: bfloat16 [16384, 14784], P('replica'), may hold values from -6 to 6
Outputs:
- new_master: float32 [14784, 4096], P('replica', 'tensor')
- new_first: float32 [14784, 4096], P('replica', 'tensor')
- new_second: float32 [14784, 4096], P('replica', 'tensor')
- decoded: bfloat16 [16384, 4096], P('replica', 'tensor')
All inputs are finite; a program needn't handle non-finite values.
Results may differ from a plain program's by a relative error of at most 0.0049.
Values may be sent and summed in bfloat16 or wider, within the bound.
A program may use at most 64 MiB of HBM per device.

v0:
```python
import math

import jax
import jax.numpy as jnp
from jax import lax
from jax.sharding import PartitionSpec as P


def per_device(train_hidden, out_grad, master, first_moment, second_moment, decode_hidden):
    tokens_all = train_hidden.shape[0]
    columns = lax.all_to_all(out_grad, "tensor", split_axis=1, concat_axis=0, tiled=True)
    grad = lax.dot_general(
        train_hidden, columns, (((0,), (0,)), ((), ())), preferred_element_type=jnp.float32
    )
    grad = grad * (1.0 / math.sqrt(tokens_all))
    new_first = 0.9 * first_moment + 0.1 * grad
    new_second = 0.95 * second_moment + 0.05 * grad * grad
    new_master = master - 0.002 * new_first / (jnp.sqrt(new_second) + 1e-08)
    weights = new_master.astype(jnp.bfloat16)
    summed = jnp.dot(
        decode_hidden,
        lax.all_gather(weights, "replica", axis=0, tiled=True),
        preferred_element_type=jnp.float32,
    )
    return (new_master, new_first, new_second, summed.astype(jnp.bfloat16))


def solution(mesh):
    placed = (
        P(None, "replica"),
        P("tensor", None),
        P("replica", "tensor"),
        P("replica", "tensor"),
        P("replica", "tensor"),
        P("replica", None),
    )
    return jax.shard_map(
        per_device,
        mesh=mesh,
        in_specs=placed,
        out_specs=(
            P("replica", "tensor"),
            P("replica", "tensor"),
            P("replica", "tensor"),
            P("replica", "tensor"),
        ),
        check_vma=False,
    )
```

profile of v0, /device:TPU:2, one launch (start us, length us, event | category | flops | bytes accessed | tf_op | source)
XLA Modules:
  0.0 361.1 jit_solution(4573648849181428409)
XLA Ops:
  7.2 0.0 copy-start
  7.2 0.0 all-gather.3.cloned.1.call-start
  7.2 1.1 copy.18
  8.4 41.3 %all_to_all.19 = bf16[64,16,256]{2,0,1:T(8,128)(2,1)S(1)} all-to-all(bf16[64,16,256]{2,0,1:T(8,128)(2,1)S(1)} %bitcast.16), channel_id=1, replica_groups=mesh['replica'=64,'tensor'=16] {'tensor'}, dimensions={1} | all-to-all | bytes 1048576 | tf_op jit(solution)/shard_map/all_to_all | solution.py:11
  49.7 0.0 copy-done
  49.7 2.5 convert_bitcast_fusion
  52.1 0.0 all-gather.3.cloned.1.call-update
  52.1 284.6 %all-gather.3.cloned.1.call-done = bf16[64,231,256]{2,1,0:T(8,128)(2,1)} async-done(((bf16[1,231,256]{2,1,0:T(8,128)(2,1)}), bf16[64,231,256]{2,1,0:T(8,128)(2,1)}) %all-gather.3.cloned.1.call-update) | async-done | bytes 7569424 | tf_op jit(solution)/shard_map/all_gather | solution.py:22
  336.7 9.3 %reshape.12 = bf16[14784,256]{1,0:T(8,128)(2,1)} reshape(bf16[64,231,256]{2,1,0:T(8,128)(2,1)} %all-gather.3.cloned.1.call-done) | data formatting | bytes 15138816
  346.0 7.5 %fusion = bf16[256,256]{0,1:T(8,128)(2,1)S(1)} fusion(bf16[14784,256]{1,0:T(8,128)(2,1)} %reshape.12, bf16[256,14784]{0,1:T(8,128)(2,1)} %param.11), kind=kOutput, calls=%fused_computation.1 | convolution fusion | flops 1937833984 | bytes 15269888 | tf_op jit(solution)/shard_map/dot_general | solution.py:20
  353.5 0.8 copy.15
Async XLA Ops:
  7.2 42.5 %copy-start = (bf16[1024,231]{0,1:T(8,128)(2,1)S(1)}, bf16[1024,231]{0,1:T(8,128)(2,1)}, u32[]{:S(2)}) copy-start(bf16[1024,231]{0,1:T(8,128)(2,1)} %param.6) | copy-start | bytes 1419268
  7.2 329.6 %all-gather.3.cloned.1.call-start = ((), (), s32[]{:S(2)}) async-start(), calls=%async_computation.1 | async-start | bytes 7720960 | tf_op jit(solution)/shard_map/all_gather | solution.py:22
Sparse Core Ops, SparseCore 0:
  52.3 284.4 all-gather.2
where the time goes:
time: 361 us
  waiting for transfers between devices  285 us (79%)
  blocking collectives  41.3 us (11%)
  between operations  14.1 us (4%)
  local copies, waits for them, and re-layouts  11.2 us (3%)
  matrix products  9.93 us (3%)
    all_gather x1, waiting for transfers between devices, per_device(): lax.all_gather(weights, 'replica', axis=0, tiled=True)  285 us
    all_to_all x1, blocking collectives, per_device(): lax.all_to_all(out_grad, 'tensor', split_axis=1, concat_axis=0, tiled=True)  41.3 us
    unnamed x4, local copies, waits for them, and re-layouts  10 us
    dot_general x1, matrix products, per_device(): jnp.dot(decode_hidden, lax.all_gather(weights, 'replica', axis=0, tiled=T...  7.48 us
  transfers between devices with their start and end apart: 1, of which 1 were waited for; matrix products, arithmetic and copies ran while one was open for 0% of the time, Pallas kernels for 0%

commit v1 on v0

v1 whole, which is shorter than its diff:
```python
import math

import jax
import jax.numpy as jnp
from jax import lax
from jax.experimental import pallas as pl
from jax.experimental.pallas import tpu as pltpu
from jax.sharding import PartitionSpec as P

MESH = pl.DeviceIdType.MESH
NX, NY, NZ = 4, 8, 16
HALF = NZ // 2
SLOT = 256
SENT = 240
CUT = 96
PARTS = ((0, CUT), (CUT, SENT - CUT))
RELAY_AFTER = 2
LAG = 4


def offsets(hops):
    out = []
    for i in (0, 1, -1, 2):
        j = hops - abs(i)
        if j == 0:
            out.append((i, 0))
        elif j > 0:
            if j <= NY // 2:
                out.append((i, j))
            if j <= NY // 2 - 1:
                out.append((i, -j))
    return out


def kernel(
    th_hbm, og_hbm, ma_hbm, fi_hbm, se_hbm, dh_hbm,
    nm_hbm, nf_hbm, ns_hbm, dec_hbm,
    th, og, cols, ma, fi, se, nm, nf, ns, wide, dh, apad, w, relay, acc, dec,
    in_sem, out_sem, col_send, col_recv, own_sem, w_send, w_recv, z_send, z_recv,
):
    r = lax.axis_index("replica")
    t = lax.axis_index("tensor")
    x, y, zh = r % NX, (r // NX) % NY, r // (NX * NY)
    zl, core = t // 2, t % 2
    z = zh * HALF + zl
    rows, width = ma.shape
    tokens_in = og.shape[0]
    tokens_all = th.shape[0]

    def device(xx, yy, zz, cc):
        return ((zz // HALF) * (NX * NY) + yy * NX + xx, (zz % HALF) * 2 + cc)

    loads = [
        pltpu.make_async_copy(a, b, in_sem.at[k])
        for k, (a, b) in enumerate(
            ((og_hbm, og), (dh_hbm, dh), (th_hbm, th), (ma_hbm, ma), (fi_hbm, fi), (se_hbm, se))
        )
    ]
    for copy in loads:
        copy.start()

    right, left = (x + 1) % NX, (x + NX - 1) % NX
    up, down = (y + 1) % NY, (y + NY - 1) % NY
    barrier = pltpu.get_barrier_semaphore()
    greeted = [device(right, y, z, core), device(left, y, z, core),
               device(x, up, z, core), device(x, down, z, core), device(x, y, z, 1 - core)]
    for d in (4, -4, 3, -3, 2, -2, 1, -1):
        for c in range(2):
            greeted.append(device(x, y, (z + d + NZ) % NZ, c))
    for d in reversed(greeted):
        pl.semaphore_signal(barrier, inc=1, device_id=d, device_id_type=MESH)
    pl.semaphore_wait(barrier, len(greeted))

    loads[0].wait()
    first = pl.multiple_of(zl * 2 * tokens_in + core * tokens_in, tokens_in)
    own = pltpu.make_async_copy(
        og.at[:, pl.ds(pl.multiple_of(t * width, width), width)],
        cols.at[pl.ds(first, tokens_in)], own_sem)
    own.start()

    def send_columns(d, c, lo, n):
        zz = (z + d + NZ) % NZ
        tt = (zz % HALF) * 2 + c
        pltpu.make_async_remote_copy(
            src_ref=og.at[pl.ds(lo, n), pl.ds(pl.multiple_of(tt * width, width), width)],
            dst_ref=cols.at[pl.ds(pl.multiple_of(first + lo, n), n)],
            send_sem=col_send, recv_sem=col_recv,
            device_id=device(x, y, zz, c), device_id_type=MESH,
        ).start()

    half = tokens_in // 2
    for c in range(2):
        send_columns(4, c, 0, half)
        send_columns(-4, c, half, half)
    for d in (3, -3, 2, -2, 1, -1):
        for c in range(2):
            send_columns(d, c, 0, tokens_in)
    send_columns(0, 1 - core, 0, tokens_in)

    wide[...] = jnp.zeros_like(wide)
    acc[...] = jnp.zeros_like(acc)

    def clear(g, carry):
        for k in range(NX):
            w[g, pl.ds(k * SLOT + SENT, SLOT - SENT), :] = jnp.zeros((SLOT - SENT, width), w.dtype)
        return carry

    lax.fori_loop(0, w.shape[0], clear, 0)
    loads[1].wait()
    strip = 64
    lane = lax.broadcasted_iota(jnp.int32, (strip, 128), 1)

    def place(b, tiles, shift, strip_at):
        turned = [pltpu.roll(v.astype(jnp.float32), (128 - shift) % 128, 1) for v in tiles]
        low = jnp.where(lane < 128 - shift, turned[0], turned[1])
        high = jnp.where(lane < 128 - shift, turned[1], turned[2])
        high = jnp.where(lane < rows - 128, high, 0.0)
        at = pl.multiple_of((b % NX) * SLOT, SLOT)
        apad[b // NX, pl.ds(strip_at, strip), pl.ds(at, 128)] = low.astype(apad.dtype)
        apad[b // NX, pl.ds(strip_at, strip), pl.ds(pl.multiple_of(at + 128, 128), 128)] = high.astype(apad.dtype)

    blocks = NX * w.shape[0]

    def relayout(b, carry):
        base = (b * rows) // 128 * 128
        shift = b * rows - base
        for s in range(0, dh.shape[0], strip):
            tiles = [dh[pl.ds(s, strip), pl.ds(pl.multiple_of(base + 128 * k, 128), 128)] for k in range(3)]
            place(b, tiles, shift, s)
        return carry

    lax.fori_loop(0, blocks - 1, relayout, 0)
    last = (blocks - 1) * rows
    tail = dh.shape[1] - last // 128 * 128 - 256
    for s in range(0, dh.shape[0], strip):
        base = last // 128 * 128
        tiles = [dh[pl.ds(s, strip), pl.ds(base + 128 * k, 128)] for k in range(2)]
        tiles.append(jnp.concatenate(
            [dh[pl.ds(s, strip), pl.ds(base + 256, tail)], jnp.zeros((strip, 128 - tail), dh.dtype)], axis=1))
        place(blocks - 1, tiles, last - base, s)

    for copy in loads[2:]:
        copy.wait()
    own.wait()
    others = tokens_all - tokens_in
    pltpu.make_async_copy(cols.at[pl.ds(0, others)], cols.at[pl.ds(0, others)], col_recv).wait()
    grad = lax.dot_general(th[...], cols[...], (((0,), (0,)), ((), ())), preferred_element_type=jnp.float32)
    grad = grad * (1.0 / math.sqrt(tokens_all))
    new_first = 0.9 * fi[...] + 0.1 * grad
    new_second = 0.95 * se[...] + 0.05 * grad * grad
    new_master = ma[...] - 0.002 * new_first / (jnp.sqrt(new_second) + 1e-08)
    wide[pl.ds(0, rows), :] = new_master

    def slot_of(ref, b, lo, n):
        return ref.at[b // NX, pl.ds(pl.multiple_of((b % NX) * SLOT + lo, 16), n)]

    w[r // NX, pl.ds(pl.multiple_of((r % NX) * SLOT, SLOT), SENT), :] = wide[pl.ds(0, SENT), :].astype(w.dtype)

    def geometry(s):
        sign = 1 - 2 * ((core + s) % 2)
        plane = (zh + s) % 2

        def block(i, j):
            xx = (x - i * sign + 2 * NX) % NX
            yy = (y - j * sign + 2 * NY) % NY
            return plane * (NX * NY) + yy * NX + xx

        def toward(axis, step):
            if axis == 0:
                return device((x + step * sign + NX) % NX, y, z, core)
            return device(x, (y + step * sign + NY) % NY, z, core)

        return block, toward

    def forward(b, part, to):
        lo, n = PARTS[part]
        pltpu.make_async_remote_copy(
            src_ref=slot_of(w, b, lo, n), dst_ref=slot_of(w, b, lo, n),
            send_sem=w_send, recv_sem=w_recv.at[b * 2 + part], device_id=to, device_id_type=MESH,
        ).start()

    def arrived(b, part):
        lo, n = PARTS[part]
        pltpu.make_async_copy(slot_of(w, b, lo, n), slot_of(w, b, lo, n), w_recv.at[b * 2 + part]).wait()

    def onward(s, i, j, part):
        block, toward = geometry(s)
        b = block(i, j)
        first_axis = 0 if part == 0 else 1
        along = (i, j)[first_axis]
        across = (i, j)[1 - first_axis]
        reach = (NX // 2, NY // 2)
        if across == 0:
            if 0 <= along < reach[first_axis]:
                forward(b, part, toward(first_axis, 1))
            if -(reach[first_axis] - 1) < along <= 0:
                forward(b, part, toward(first_axis, -1))
        if 0 <= across < reach[1 - first_axis]:
            forward(b, part, toward(1 - first_axis, 1))
        if -(reach[1 - first_axis] - 1) < across <= 0:
            forward(b, part, toward(1 - first_axis, -1))

    def wave(s, hops):
        block, _ = geometry(s)
        for i, j in offsets(hops):
            for part in ((1, 0) if i == 0 else (0, 1)):
                arrived(block(i, j), part)
                onward(s, i, j, part)

    def multiply(s, j):
        block, _ = geometry(s)
        g = block(0, j) // NX
        acc[...] += jnp.dot(apad[g], w[g], preferred_element_type=jnp.float32)

    def multiply_after(s, hops):
        j = hops - 2
        if j == 0:
            multiply(s, 0)
        elif 0 < j < NY // 2:
            def both(k, carry):
                multiply(s, j * (1 - 2 * k))
                return carry
            lax.fori_loop(0, 2, both, 0)
        elif j == NY // 2:
            multiply(s, j)

    zs = 4 * (1 - 2 * core)
    steps = (zs, -zs)
    for part, (lo, n) in enumerate(PARTS):
        pltpu.make_async_remote_copy(
            src_ref=slot_of(w, r, lo, n), dst_ref=relay.at[pl.ds(lo, n)],
            send_sem=z_send.at[part], recv_sem=z_recv.at[part],
            device_id=device(x, y, (z + steps[part] + NZ) % NZ, core), device_id_type=MESH,
        ).start()
    for part in (1, 0):
        onward(0, 0, 0, part)
    outs = [
        pltpu.make_async_copy(a, b, out_sem.at[k])
        for k, (a, b) in enumerate(((nm, nm_hbm), (nf, nf_hbm), (ns, ns_hbm)))
    ]
    nm[...] = new_master
    nf[...] = new_first
    ns[...] = new_second
    for copy in outs:
        copy.start()

    def serve_relay():
        for part, (lo, n) in enumerate(PARTS):
            origin = (z - steps[part] + NZ) % NZ
            target = (z + steps[part] + NZ) % NZ
            b = (origin // HALF) * (NX * NY) + y * NX + x
            pltpu.make_async_copy(relay.at[pl.ds(lo, n)], relay.at[pl.ds(lo, n)], z_recv.at[part]).wait()
            pltpu.make_async_remote_copy(
                src_ref=relay.at[pl.ds(lo, n)], dst_ref=slot_of(w, b, lo, n),
                send_sem=z_send.at[2 + part], recv_sem=w_recv.at[b * 2 + part],
                device_id=device(x, y, target, core), device_id_type=MESH,
            ).start()

    far = NX // 2 + NY // 2
    for hops in range(1, far + LAG):
        if hops == LAG:
            block, _ = geometry(1)
            for part in (1, 0):
                arrived(block(0, 0), part)
                onward(1, 0, 0, part)
        if hops <= far:
            wave(0, hops)
        if hops == RELAY_AFTER:
            serve_relay()
        if 1 <= hops - LAG + 1 <= far and hops >= LAG:
            wave(1, hops - LAG + 1)
        if hops <= far:
            multiply_after(0, hops)
        if hops >= LAG:
            multiply_after(1, hops - LAG + 1)

    dec[...] = acc[...].astype(dec.dtype)
    final = pltpu.make_async_copy(dec, dec_hbm, out_sem.at[3])
    final.start()

    pltpu.make_async_copy(cols.at[pl.ds(0, others)], cols.at[pl.ds(0, others)], col_send).wait()
    for k in range(4):
        lo, n = PARTS[k % 2]
        pltpu.make_async_copy(relay.at[pl.ds(lo, n)], relay.at[pl.ds(lo, n)], z_send.at[k]).wait()
    window = w.at[pl.ds(0, 2 * NY - 1), pl.ds(0, 2 * (NX * NY - 1) * SENT // (2 * NY - 1))]
    pltpu.make_async_copy(window, window, w_send).wait()
    for copy in outs:
        copy.wait()
    final.wait()


def per_device(train_hidden, out_grad, master, first_moment, second_moment, decode_hidden):
    rows, width = master.shape
    tokens_all = train_hidden.shape[0]
    lines = decode_hidden.shape[0]
    f32, bf16 = jnp.float32, jnp.bfloat16
    any_spec = pl.BlockSpec(memory_space=pl.ANY)
    block = jax.ShapeDtypeStruct((rows, width), f32)
    groups = 2 * NY
    return pl.pallas_call(
        kernel,
        out_shape=(block, block, block, jax.ShapeDtypeStruct((lines, width), bf16)),
        in_specs=[any_spec] * 6,
        out_specs=(any_spec,) * 4,
        scratch_shapes=[
            pltpu.VMEM(train_hidden.shape, bf16),
            pltpu.VMEM(out_grad.shape, bf16),
            pltpu.VMEM((tokens_all, width), bf16),
            pltpu.VMEM((rows, width), f32),
            pltpu.VMEM((rows, width), f32),
            pltpu.VMEM((rows, width), f32),
            pltpu.VMEM((rows, width), f32),
            pltpu.VMEM((rows, width), f32),
            pltpu.VMEM((rows, width), f32),
            pltpu.VMEM((SLOT, width), f32),
            pltpu.VMEM(decode_hidden.shape, bf16),
            pltpu.VMEM((groups, lines, NX * SLOT), bf16),
            pltpu.VMEM((groups, NX * SLOT, width), bf16),
            pltpu.VMEM((SENT, width), bf16),
            pltpu.VMEM((lines, width), f32),
            pltpu.VMEM((lines, width), bf16),
            pltpu.SemaphoreType.DMA((6,)),
            pltpu.SemaphoreType.DMA((4,)),
            pltpu.SemaphoreType.DMA,
            pltpu.SemaphoreType.DMA,
            pltpu.SemaphoreType.DMA,
            pltpu.SemaphoreType.DMA,
            pltpu.SemaphoreType.DMA((2 * NX * groups,)),
            pltpu.SemaphoreType.DMA((4,)),
            pltpu.SemaphoreType.DMA((2,)),
        ],
        compiler_params=pltpu.CompilerParams(
            collective_id=0, has_side_effects=True, vmem_limit_bytes=60 * 1024 * 1024
        ),
    )(train_hidden, out_grad, master, first_moment, second_moment, decode_hidden)


def solution(mesh):
    placed = (
        P(None, "replica"),
        P("tensor", None),
        P("replica", "tensor"),
        P("replica", "tensor"),
        P("replica", "tensor"),
        P("replica", None),
    )
    return jax.shard_map(
        per_device,
        mesh=mesh,
        in_specs=placed,
        out_specs=(
            P("replica", "tensor"),
            P("replica", "tensor"),
            P("replica", "tensor"),
            P("replica", "tensor"),
        ),
        check_vma=False,
    )
```

time: 361 us -> 107 us (0.30)
  the two profiles are of different devices: /device:TPU:2 before, /device:TPU:8 now
where the time goes in v1:
time: 107 us; the launch traced here: 106 us
  Pallas kernels  86.9 us (81%)
  local copies, waits for them, and re-layouts  18.7 us (17%)
    pallas_call x1, Pallas kernels, per_device(): pl.pallas_call(kernel, out_shape=(block, block, block, jax.ShapeDtypeStru...  86.9 us
    unnamed x6, local copies, waits for them, and re-layouts  18.7 us

profile of v1, /device:TPU:8, one launch (start us, length us, event | category | flops | bytes accessed | tf_op | source)
XLA Modules:
  0.0 106.3 jit_solution(16762171892980168253)
XLA Ops:
  0.6 2.0 %copy.10.th_hbm = bf16[1024,231]{1,0:T(8,128)(2,1)} copy(bf16[1024,231]{0,1:T(8,128)(2,1)} %param.6) | data formatting | bytes 946176 | tf_op args[0]
  2.7 10.2 %copy.11.dh_hbm = bf16[256,14784]{1,0:T(8,128)(2,1)} copy(bf16[256,14784]{0,1:T(8,128)(2,1)} %param.11) | data formatting | bytes 15138816 | tf_op args[5]
  12.8 86.9 %shard_map.93 = (f32[231,256]{1,0:T(8,128)}, f32[231,256]{1,0:T(8,128)}, f32[231,256]{1,0:T(8,128)}, bf16[256,256]{1,0:T(8,128)(2,1)}) custom-call(bf16[1024,231]{1,0:T(8,128)(2,1)} %copy.10.th_hbm, bf16[64,4096]{1,0:T(8,128)(2,1)} %og_hbm.1, f32[231,256]{1,0:T(8,128)} %ma_hbm.1, f32[231,256]{1,0:T(8,128)} %fi_hbm.1, f32[231,256]{1,0:T(8,128)} %se_hbm.1, ...), custom_call_target="tpu_custom_call" | custom-call | tf_op jit(solution)/shard_map/pallas_call | solution.py:300
  99.8 1.6 %copy.16 = f32[231,256]{1,0:T(8,128)} copy(f32[231,256]{1,0:T(8,128)} %get-tuple-element.8) | data formatting | bytes 473088
  101.4 1.6 %copy.17 = f32[231,256]{1,0:T(8,128)} copy(f32[231,256]{1,0:T(8,128)} %get-tuple-element.9) | data formatting | bytes 473088
  103.1 1.6 %copy.18 = f32[231,256]{1,0:T(8,128)} copy(f32[231,256]{1,0:T(8,128)} %get-tuple-element.10) | data formatting | bytes 473088
  104.7 1.6 %copy.19 = bf16[256,256]{1,0:T(8,128)(2,1)} copy(bf16[256,256]{1,0:T(8,128)(2,1)} %get-tuple-element.11) | data formatting | bytes 262144

commit v2 on v1

--- a/solution.py
+++ b/solution.py
@@ -14,7 +14,7 @@
 SENT = 240
 CUT = 96
 PARTS = ((0, CUT), (CUT, SENT - CUT))
-RELAY_AFTER = 2
+RELAY_AFTER = 1
 LAG = 4
 
 
@@ -45,7 +45,7 @@
     z = zh * HALF + zl
     rows, width = ma.shape
     tokens_in = og.shape[0]
-    tokens_all = th.shape[0]
+    tokens_all = th.shape[1]
 
     def device(xx, yy, zz, cc):
         return ((zz // HALF) * (NX * NY) + yy * NX + xx, (zz % HALF) * 2 + cc)
@@ -53,7 +53,7 @@
     loads = [
         pltpu.make_async_copy(a, b, in_sem.at[k])
         for k, (a, b) in enumerate(
-            ((og_hbm, og), (dh_hbm, dh), (th_hbm, th), (ma_hbm, ma), (fi_hbm, fi), (se_hbm, se))
+            ((og_hbm, og), (dh_hbm, dh.at[pl.ds(0, dh_hbm.shape[0])]), (th_hbm, th), (ma_hbm, ma), (fi_hbm, fi), (se_hbm, se))
         )
     ]
     for copy in loads:
@@ -107,44 +107,29 @@
 
     lax.fori_loop(0, w.shape[0], clear, 0)
     loads[1].wait()
-    strip = 64
-    lane = lax.broadcasted_iota(jnp.int32, (strip, 128), 1)
-
-    def place(b, tiles, shift, strip_at):
-        turned = [pltpu.roll(v.astype(jnp.float32), (128 - shift) % 128, 1) for v in tiles]
-        low = jnp.where(lane < 128 - shift, turned[0], turned[1])
-        high = jnp.where(lane < 128 - shift, turned[1], turned[2])
-        high = jnp.where(lane < rows - 128, high, 0.0)
+    lane = lax.broadcasted_iota(jnp.int32, (128, 128), 1)
+
+    def relayout(b, carry):
+        base = pl.multiple_of((b * rows) // 16 * 16, 16)
+        shift = b * rows - base
         at = pl.multiple_of((b % NX) * SLOT, SLOT)
-        apad[b // NX, pl.ds(strip_at, strip), pl.ds(at, 128)] = low.astype(apad.dtype)
-        apad[b // NX, pl.ds(strip_at, strip), pl.ds(pl.multiple_of(at + 128, 128), 128)] = high.astype(apad.dtype)
-
-    blocks = NX * w.shape[0]
-
-    def relayout(b, carry):
-        base = (b * rows) // 128 * 128
-        shift = b * rows - base
-        for s in range(0, dh.shape[0], strip):
-            tiles = [dh[pl.ds(s, strip), pl.ds(pl.multiple_of(base + 128 * k, 128), 128)] for k in range(3)]
-            place(b, tiles, shift, s)
+        for s in range(0, dh.shape[1], 128):
+            tile = dh[pl.ds(base, SLOT), pl.ds(s, 128)].T.astype(jnp.float32)
+            turned = [pltpu.roll(tile[:, k * 128 : k * 128 + 128], (128 - shift) % 128, 1) for k in range(2)]
+            low = jnp.where(lane < 128 - shift, turned[0], turned[1])
+            high = jnp.where(lane < rows - 128, turned[1], 0.0)
+            apad[b // NX, pl.ds(s, 128), pl.ds(at, 128)] = low.astype(apad.dtype)
+            apad[b // NX, pl.ds(s, 128), pl.ds(pl.multiple_of(at + 128, 128), 128)] = high.astype(apad.dtype)
         return carry
 
-    lax.fori_loop(0, blocks - 1, relayout, 0)
-    last = (blocks - 1) * rows
-    tail = dh.shape[1] - last // 128 * 128 - 256
-    for s in range(0, dh.shape[0], strip):
-        base = last // 128 * 128
-        tiles = [dh[pl.ds(s, strip), pl.ds(base + 128 * k, 128)] for k in range(2)]
-        tiles.append(jnp.concatenate(
-            [dh[pl.ds(s, strip), pl.ds(base + 256, tail)], jnp.zeros((strip, 128 - tail), dh.dtype)], axis=1))
-        place(blocks - 1, tiles, last - base, s)
+    lax.fori_loop(0, NX * w.shape[0], relayout, 0)
 
     for copy in loads[2:]:
         copy.wait()
     own.wait()
     others = tokens_all - tokens_in
     pltpu.make_async_copy(cols.at[pl.ds(0, others)], cols.at[pl.ds(0, others)], col_recv).wait()
-    grad = lax.dot_general(th[...], cols[...], (((0,), (0,)), ((), ())), preferred_element_type=jnp.float32)
+    grad = jnp.dot(th[...], cols[...], preferred_element_type=jnp.float32)
     grad = grad * (1.0 / math.sqrt(tokens_all))
     new_first = 0.9 * fi[...] + 0.1 * grad
     new_second = 0.95 * se[...] + 0.05 * grad * grad
@@ -289,6 +274,11 @@
     final.wait()
 
 
+def hand_on(*refs):
+    for source, target in zip(refs[:4], refs[4:]):
+        target[...] = source[...]
+
+
 def per_device(train_hidden, out_grad, master, first_moment, second_moment, decode_hidden):
     rows, width = master.shape
     tokens_all = train_hidden.shape[0]
@@ -297,13 +287,13 @@
     any_spec = pl.BlockSpec(memory_space=pl.ANY)
     block = jax.ShapeDtypeStruct((rows, width), f32)
     groups = 2 * NY
-    return pl.pallas_call(
+    results = pl.pallas_call(
         kernel,
         out_shape=(block, block, block, jax.ShapeDtypeStruct((lines, width), bf16)),
         in_specs=[any_spec] * 6,
         out_specs=(any_spec,) * 4,
         scratch_shapes=[
-            pltpu.VMEM(train_hidden.shape, bf16),
+            pltpu.VMEM((rows, tokens_all), bf16),
             pltpu.VMEM(out_grad.shape, bf16),
             pltpu.VMEM((tokens_all, width), bf16),
             pltpu.VMEM((rows, width), f32),
@@ -313,7 +303,7 @@
             pltpu.VMEM((rows, width), f32),
             pltpu.VMEM((rows, width), f32),
             pltpu.VMEM((SLOT, width), f32),
-            pltpu.VMEM(decode_hidden.shape, bf16),
+            pltpu.VMEM((decode_hidden.shape[1] + 16, lines), bf16),
             pltpu.VMEM((groups, lines, NX * SLOT), bf16),
             pltpu.VMEM((groups, NX * SLOT, width), bf16),
             pltpu.VMEM((SENT, width), bf16),
@@ -332,7 +322,11 @@
         compiler_params=pltpu.CompilerParams(
             collective_id=0, has_side_effects=True, vmem_limit_bytes=60 * 1024 * 1024
         ),
-    )(train_hidden, out_grad, master, first_moment, second_moment, decode_hidden)
+    )(train_hidden.T, out_grad, master, first_moment, second_moment, decode_hidden.T)
+    return pl.pallas_call(
+        hand_on,
+        out_shape=tuple(jax.ShapeDtypeStruct(a.shape, a.dtype) for a in results),
+    )(*results)
 
 
 def solution(mesh):

time: 107 us -> 89.3 us (0.83)
  local copies, waits for them, and re-layouts: 18.7 us -> 0 us
  Pallas kernels: 86.9 us -> 88.5 us
    unnamed x6 -> x0, local copies, waits for them, and re-layouts: 18.7 us -> none
    pallas_call x0 -> x1, Pallas kernels: none -> 2.16 us  [per_device(): pl.pallas_call(hand_on, out_shape=tuple((jax.ShapeDtypeStruct(a.shape, a....]
where the time goes in v2:
time: 89.3 us; the launch traced here: 89.1 us
  Pallas kernels  88.5 us (99%)
    pallas_call x1, Pallas kernels, per_device(): pl.pallas_call(kernel, out_shape=(block, block, block, jax.ShapeDtypeStru...  86.3 us
    pallas_call x1, Pallas kernels, per_device(): pl.pallas_call(hand_on, out_shape=tuple((jax.ShapeDtypeStruct(a.shape, a....  2.16 us

profile of v2, /device:TPU:8, one launch (start us, length us, event | category | flops | bytes accessed | tf_op | source)
XLA Modules:
  0.0 89.1 jit_solution(9257792906312258517)
XLA Ops:
  0.6 86.3 %shard_map.93 = (f32[231,256]{1,0:T(8,128)}, f32[231,256]{1,0:T(8,128)}, f32[231,256]{1,0:T(8,128)}, bf16[256,256]{1,0:T(8,128)(2,1)}) custom-call(bf16[231,1024]{1,0:T(8,128)(2,1)} %bitcast.3, bf16[64,4096]{1,0:T(8,128)(2,1)} %og_hbm.1, f32[231,256]{1,0:T(8,128)} %ma_hbm.1, f32[231,256]{1,0:T(8,128)} %fi_hbm.1, f32[231,256]{1,0:T(8,128)} %se_hbm.1, ...), custom_call_target="tpu_custom_call" | custom-call | tf_op jit(solution)/shard_map/pallas_call | solution.py:290
  87.0 2.2 %shard_map.94 = (f32[231,256]{1,0:T(8,128)}, f32[231,256]{1,0:T(8,128)}, f32[231,256]{1,0:T(8,128)}, bf16[256,256]{1,0:T(8,128)(2,1)}) custom-call(f32[231,256]{1,0:T(8,128)} %get-tuple-element.8.refs_0_, f32[231,256]{1,0:T(8,128)} %get-tuple-element.9.refs_1_, f32[231,256]{1,0:T(8,128)} %get-tuple-element.10.refs_2_, bf16[256,256]{1,0:T(8,128)(2,1)} %get-tuple-element.11.refs_3_), custom_call_target="tpu_custom_call" | custom-call | tf_op jit(solution)/shard_map/pallas_call | solution.py:326

commit v3 on v2

--- a/solution.py
+++ b/solution.py
@@ -11,11 +11,11 @@
 NX, NY, NZ = 4, 8, 16
 HALF = NZ // 2
 SLOT = 256
-SENT = 240
+SENT = 232
 CUT = 96
 PARTS = ((0, CUT), (CUT, SENT - CUT))
 RELAY_AFTER = 1
-LAG = 4
+LAG = 5
 
 
 def offsets(hops):
@@ -36,7 +36,7 @@
     th_hbm, og_hbm, ma_hbm, fi_hbm, se_hbm, dh_hbm,
     nm_hbm, nf_hbm, ns_hbm, dec_hbm,
     th, og, cols, ma, fi, se, nm, nf, ns, wide, dh, apad, w, relay, acc, dec,
-    in_sem, out_sem, col_send, col_recv, own_sem, w_send, w_recv, z_send, z_recv,
+    in_sem, out_sem, col_send, col_recv, x_send, x_recv, own_sem, everyone, w_send, w_recv, z_send, z_recv,
 ):
     r = lax.axis_index("replica")
     t = lax.axis_index("tensor")
@@ -64,52 +64,16 @@
     barrier = pltpu.get_barrier_semaphore()
     greeted = [device(right, y, z, core), device(left, y, z, core),
                device(x, up, z, core), device(x, down, z, core), device(x, y, z, 1 - core)]
-    for d in (4, -4, 3, -3, 2, -2, 1, -1):
+    for d in range(1, HALF):
+        zz = zh * HALF + (zl + d) % HALF
         for c in range(2):
-            greeted.append(device(x, y, (z + d + NZ) % NZ, c))
-    for d in reversed(greeted):
+            greeted.append(device(x, y, zz, c))
+    for d in greeted:
         pl.semaphore_signal(barrier, inc=1, device_id=d, device_id_type=MESH)
-    pl.semaphore_wait(barrier, len(greeted))
-
-    loads[0].wait()
-    first = pl.multiple_of(zl * 2 * tokens_in + core * tokens_in, tokens_in)
-    own = pltpu.make_async_copy(
-        og.at[:, pl.ds(pl.multiple_of(t * width, width), width)],
-        cols.at[pl.ds(first, tokens_in)], own_sem)
-    own.start()
-
-    def send_columns(d, c, lo, n):
-        zz = (z + d + NZ) % NZ
-        tt = (zz % HALF) * 2 + c
-        pltpu.make_async_remote_copy(
-            src_ref=og.at[pl.ds(lo, n), pl.ds(pl.multiple_of(tt * width, width), width)],
-            dst_ref=cols.at[pl.ds(pl.multiple_of(first + lo, n), n)],
-            send_sem=col_send, recv_sem=col_recv,
-            device_id=device(x, y, zz, c), device_id_type=MESH,
-        ).start()
-
-    half = tokens_in // 2
-    for c in range(2):
-        send_columns(4, c, 0, half)
-        send_columns(-4, c, half, half)
-    for d in (3, -3, 2, -2, 1, -1):
-        for c in range(2):
-            send_columns(d, c, 0, tokens_in)
-    send_columns(0, 1 - core, 0, tokens_in)
-
-    wide[...] = jnp.zeros_like(wide)
-    acc[...] = jnp.zeros_like(acc)
-
-    def clear(g, carry):
-        for k in range(NX):
-            w[g, pl.ds(k * SLOT + SENT, SLOT - SENT), :] = jnp.zeros((SLOT - SENT, width), w.dtype)
-        return carry
-
-    lax.fori_loop(0, w.shape[0], clear, 0)
-    loads[1].wait()
+
     lane = lax.broadcasted_iota(jnp.int32, (128, 128), 1)
 
-    def relayout(b, carry):
+    def relayout(b):
         base = pl.multiple_of((b * rows) // 16 * 16, 16)
         shift = b * rows - base
         at = pl.multiple_of((b % NX) * SLOT, SLOT)
@@ -120,16 +84,95 @@
             high = jnp.where(lane < rows - 128, turned[1], 0.0)
             apad[b // NX, pl.ds(s, 128), pl.ds(at, 128)] = low.astype(apad.dtype)
             apad[b // NX, pl.ds(s, 128), pl.ds(pl.multiple_of(at + 128, 128), 128)] = high.astype(apad.dtype)
+
+    def relayout_plane(plane, lo, n):
+        def one(k, carry):
+            relayout(plane * (NX * NY) + lo + k)
+            return carry
+        lax.fori_loop(0, n, one, 0)
+
+    def clear(g, carry):
+        for k in range(NX):
+            w[g, pl.ds(k * SLOT + SENT, SLOT - SENT), :] = jnp.zeros((SLOT - SENT, width), w.dtype)
         return carry
 
-    lax.fori_loop(0, NX * w.shape[0], relayout, 0)
+    def prepare():
+        loads[1].wait()
+        lax.fori_loop(0, w.shape[0], clear, 0)
+        relayout_plane(zh, 0, NX * NY)
+
+    early = (z < HALF // 2) | (z == HALF)
+    pl.when(early)(prepare)
+
+    pl.semaphore_wait(barrier, len(greeted) + (z == HALF).astype(jnp.int32))
+
+    @pl.when(z == HALF - 1)
+    def _():
+        pl.semaphore_signal(barrier, inc=1, device_id=device(x, y, HALF, core), device_id_type=MESH)
+
+    @pl.when(z == HALF)
+    def _():
+        for d in range(1, NZ):
+            pl.semaphore_signal(everyone, inc=1, device_id=device(x, y, (HALF + d) % NZ, core), device_id_type=MESH)
+
+    loads[0].wait()
+    quarter = tokens_in // NX
+    mine = pl.ds(pl.multiple_of(x * quarter, quarter), quarter)
+    own = pltpu.make_async_copy(og.at[mine, pl.ds(pl.multiple_of(t * width, width), width)], cols.at[t, mine], own_sem)
+    own.start()
+
+    def send_columns(d, c):
+        zz = zh * HALF + (zl + d) % HALF
+        tt = (zz % HALF) * 2 + c
+        pltpu.make_async_remote_copy(
+            src_ref=og.at[mine, pl.ds(pl.multiple_of(tt * width, width), width)],
+            dst_ref=cols.at[t, mine],
+            send_sem=col_send, recv_sem=col_recv,
+            device_id=device(x, y, zz, c), device_id_type=MESH,
+        ).start()
+
+    for d in range(1, HALF):
+        for c in range(2):
+            send_columns(HALF - d, c)
+    send_columns(0, 1 - core)
+
+    wide[...] = jnp.zeros_like(wide)
+    acc[...] = jnp.zeros_like(acc)
+    pl.when(jnp.logical_not(early))(prepare)
+
+    own.wait()
+    peers = cols.at[pl.ds(0, cols.shape[0] - 1), pl.ds(0, quarter)]
+    pltpu.make_async_copy(peers, peers, col_recv).wait()
+
+    def quarters(xx, lo, n):
+        return cols.at[pl.ds(lo, n), pl.ds(pl.multiple_of(xx * quarter, quarter), quarter)]
+
+    sources = cols.shape[0]
+    half = sources // 2
+
+    def pass_on(xx, lo, n, to, k):
+        pltpu.make_async_remote_copy(
+            src_ref=quarters(xx, lo, n), dst_ref=quarters(xx, lo, n),
+            send_sem=x_send.at[k], recv_sem=x_recv.at[k],
+            device_id=device(to, y, z, core), device_id_type=MESH,
+        ).start()
+
+    def passed(xx, lo, n, sem):
+        pltpu.make_async_copy(quarters(xx, lo, n), quarters(xx, lo, n), sem).wait()
+
+    opposite = (x + 2) % NX
+    pass_on(x, 0, sources, right, 0)
+    pass_on(x, 0, sources, left, 1)
+    passed(left, 0, sources, x_recv.at[0])
+    pass_on(left, 0, half, right, 2)
+    passed(right, 0, sources, x_recv.at[1])
+    pass_on(right, half, half, left, 3)
 
     for copy in loads[2:]:
         copy.wait()
-    own.wait()
-    others = tokens_all - tokens_in
-    pltpu.make_async_copy(cols.at[pl.ds(0, others)], cols.at[pl.ds(0, others)], col_recv).wait()
-    grad = jnp.dot(th[...], cols[...], preferred_element_type=jnp.float32)
+    passed(opposite, 0, half, x_recv.at[2])
+    passed(opposite, half, half, x_recv.at[3])
+    grad = jnp.dot(th[...], cols[...].reshape(tokens_all, width), preferred_element_type=jnp.float32)
     grad = grad * (1.0 / math.sqrt(tokens_all))
     new_first = 0.9 * fi[...] + 0.1 * grad
     new_second = 0.95 * se[...] + 0.05 * grad * grad
@@ -209,6 +252,13 @@
         elif j == NY // 2:
             multiply(s, j)
 
+    for part in (1, 0):
+        onward(0, 0, 0, part)
+
+    @pl.when(z != HALF)
+    def _():
+        pl.semaphore_wait(everyone, 1)
+
     zs = 4 * (1 - 2 * core)
     steps = (zs, -zs)
     for part, (lo, n) in enumerate(PARTS):
@@ -217,8 +267,6 @@
             send_sem=z_send.at[part], recv_sem=z_recv.at[part],
             device_id=device(x, y, (z + steps[part] + NZ) % NZ, core), device_id_type=MESH,
         ).start()
-    for part in (1, 0):
-        onward(0, 0, 0, part)
     outs = [
         pltpu.make_async_copy(a, b, out_sem.at[k])
         for k, (a, b) in enumerate(((nm, nm_hbm), (nf, nf_hbm), (ns, ns_hbm)))
@@ -256,6 +304,8 @@
             wave(1, hops - LAG + 1)
         if hops <= far:
             multiply_after(0, hops)
+        if 2 <= hops < 2 + NY // 2:
+            relayout_plane(1 - zh, (hops - 2) * 2 * NX, 2 * NX)
         if hops >= LAG:
             multiply_after(1, hops - LAG + 1)
 
@@ -263,11 +313,13 @@
     final = pltpu.make_async_copy(dec, dec_hbm, out_sem.at[3])
     final.start()
 
-    pltpu.make_async_copy(cols.at[pl.ds(0, others)], cols.at[pl.ds(0, others)], col_send).wait()
+    pltpu.make_async_copy(peers, peers, col_send).wait()
+    for k, n in enumerate((sources, sources, half, half)):
+        passed(0, 0, n, x_send.at[k])
     for k in range(4):
         lo, n = PARTS[k % 2]
         pltpu.make_async_copy(relay.at[pl.ds(lo, n)], relay.at[pl.ds(lo, n)], z_send.at[k]).wait()
-    window = w.at[pl.ds(0, 2 * NY - 1), pl.ds(0, 2 * (NX * NY - 1) * SENT // (2 * NY - 1))]
+    window = dh.at[pl.ds(0, 2 * (NX * NY - 1) * SENT)]
     pltpu.make_async_copy(window, window, w_send).wait()
     for copy in outs:
         copy.wait()
@@ -295,7 +347,7 @@
         scratch_shapes=[
             pltpu.VMEM((rows, tokens_all), bf16),
             pltpu.VMEM(out_grad.shape, bf16),
-            pltpu.VMEM((tokens_all, width), bf16),
+            pltpu.VMEM((tokens_all // out_grad.shape[0], out_grad.shape[0], width), bf16),
             pltpu.VMEM((rows, width), f32),
             pltpu.VMEM((rows, width), f32),
             pltpu.VMEM((rows, width), f32),
@@ -313,7 +365,10 @@
             pltpu.SemaphoreType.DMA((4,)),
             pltpu.SemaphoreType.DMA,
             pltpu.SemaphoreType.DMA,
+            pltpu.SemaphoreType.DMA((4,)),
+            pltpu.SemaphoreType.DMA((4,)),
             pltpu.SemaphoreType.DMA,
+            pltpu.SemaphoreType.REGULAR,
             pltpu.SemaphoreType.DMA,
             pltpu.SemaphoreType.DMA((2 * NX * groups,)),
             pltpu.SemaphoreType.DMA((4,)),

time: 89.3 us -> 94.3 us (1.056)
  the two profiles are of different devices: /device:TPU:8 before, /device:TPU:72 now
where the time goes in v3:
time: 94.3 us; the launch traced here: 94.1 us
  Pallas kernels  93.5 us (99%)
    pallas_call x1, Pallas kernels, per_device(): pl.pallas_call(kernel, out_shape=(block, block, block, jax.ShapeDtypeStru...  91.3 us
    pallas_call x1, Pallas kernels, per_device(): pl.pallas_call(hand_on, out_shape=tuple((jax.ShapeDtypeStruct(a.shape, a....  2.16 us

profile of v3, /device:TPU:72, one launch (start us, length us, event | category | flops | bytes accessed | tf_op | source)
XLA Modules:
  0.0 94.1 jit_solution(17911520811117403525)
XLA Ops:
  0.6 91.3 %shard_map.93 = (f32[231,256]{1,0:T(8,128)}, f32[231,256]{1,0:T(8,128)}, f32[231,256]{1,0:T(8,128)}, bf16[256,256]{1,0:T(8,128)(2,1)}) custom-call(bf16[231,1024]{1,0:T(8,128)(2,1)} %bitcast.3, bf16[64,4096]{1,0:T(8,128)(2,1)} %og_hbm.1, f32[231,256]{1,0:T(8,128)} %ma_hbm.1, f32[231,256]{1,0:T(8,128)} %fi_hbm.1, f32[231,256]{1,0:T(8,128)} %se_hbm.1, ...), custom_call_target="tpu_custom_call" | custom-call | tf_op jit(solution)/shard_map/pallas_call | solution.py:342
  91.9 2.2 %shard_map.94 = (f32[231,256]{1,0:T(8,128)}, f32[231,256]{1,0:T(8,128)}, f32[231,256]{1,0:T(8,128)}, bf16[256,256]{1,0:T(8,128)(2,1)}) custom-call(f32[231,256]{1,0:T(8,128)} %get-tuple-element.8.refs_0_, f32[231,256]{1,0:T(8,128)} %get-tuple-element.9.refs_1_, f32[231,256]{1,0:T(8,128)} %get-tuple-element.10.refs_2_, bf16[256,256]{1,0:T(8,128)(2,1)} %get-tuple-element.11.refs_3_), custom_call_target="tpu_custom_call" | custom-call | tf_op jit(solution)/shard_map/pallas_call | solution.py:381

commit v4 on v3

--- a/solution.py
+++ b/solution.py
@@ -36,7 +36,7 @@
     th_hbm, og_hbm, ma_hbm, fi_hbm, se_hbm, dh_hbm,
     nm_hbm, nf_hbm, ns_hbm, dec_hbm,
     th, og, cols, ma, fi, se, nm, nf, ns, wide, dh, apad, w, relay, acc, dec,
-    in_sem, out_sem, col_send, col_recv, x_send, x_recv, own_sem, everyone, w_send, w_recv, z_send, z_recv,
+    in_sem, out_sem, col_send, col_recv, x_send, x_recv, own_sem, upper_in, up_send, w_send, w_recv, z_send, z_recv,
 ):
     r = lax.axis_index("replica")
     t = lax.axis_index("tensor")
@@ -64,12 +64,25 @@
     barrier = pltpu.get_barrier_semaphore()
     greeted = [device(right, y, z, core), device(left, y, z, core),
                device(x, up, z, core), device(x, down, z, core), device(x, y, z, 1 - core)]
-    for d in range(1, HALF):
-        zz = zh * HALF + (zl + d) % HALF
-        for c in range(2):
-            greeted.append(device(x, y, zz, c))
+    lower = z < HALF
+    upper = z >= HALF
+    near = [(k, d, c) for k, d in enumerate((4, -4, 3, -3, 2, -2, 1, -1)) for c in range(2)]
+
+    def along(d):
+        return (z + d + NZ) % NZ
+
     for d in greeted:
         pl.semaphore_signal(barrier, inc=1, device_id=d, device_id_type=MESH)
+    for k, d, c in near:
+        @pl.when(along(d) >= HALF)
+        def _():
+            pl.semaphore_signal(barrier, inc=1, device_id=device(x, y, along(d), c), device_id_type=MESH)
+
+    @pl.when(lower)
+    def _():
+        for d in range(1, HALF):
+            for c in range(2):
+                pl.semaphore_signal(barrier, inc=1, device_id=device(x, y, (z + d) % HALF, c), device_id_type=MESH)
 
     lane = lax.broadcasted_iota(jnp.int32, (128, 128), 1)
 
@@ -101,29 +114,25 @@
         lax.fori_loop(0, w.shape[0], clear, 0)
         relayout_plane(zh, 0, NX * NY)
 
-    early = (z < HALF // 2) | (z == HALF)
+    early = z < HALF // 2
     pl.when(early)(prepare)
 
-    pl.semaphore_wait(barrier, len(greeted) + (z == HALF).astype(jnp.int32))
-
-    @pl.when(z == HALF - 1)
-    def _():
-        pl.semaphore_signal(barrier, inc=1, device_id=device(x, y, HALF, core), device_id_type=MESH)
-
-    @pl.when(z == HALF)
-    def _():
-        for d in range(1, NZ):
-            pl.semaphore_signal(everyone, inc=1, device_id=device(x, y, (HALF + d) % NZ, core), device_id_type=MESH)
+    pl.semaphore_wait(barrier, len(greeted) + 2 * jnp.where(lower, HALF - 1, HALF))
+    for k, d, c in near:
+        @pl.when(upper & (along(d) < HALF))
+        def _():
+            pl.semaphore_signal(upper_in, inc=1, device_id=device(x, y, along(d), c), device_id_type=MESH)
 
     loads[0].wait()
     quarter = tokens_in // NX
     mine = pl.ds(pl.multiple_of(x * quarter, quarter), quarter)
-    own = pltpu.make_async_copy(og.at[mine, pl.ds(pl.multiple_of(t * width, width), width)], cols.at[t, mine], own_sem)
-    own.start()
-
-    def send_columns(d, c):
-        zz = zh * HALF + (zl + d) % HALF
-        tt = (zz % HALF) * 2 + c
+    own_columns = pl.ds(pl.multiple_of(t * width, width), width)
+    own_part = pltpu.make_async_copy(og.at[mine, own_columns], cols.at[t, mine], own_sem)
+    own_all = pltpu.make_async_copy(og.at[:, own_columns], cols.at[t], own_sem)
+
+    def send_quarter(d, c):
+        zz = (z + d) % HALF
+        tt = zz * 2 + c
         pltpu.make_async_remote_copy(
             src_ref=og.at[mine, pl.ds(pl.multiple_of(tt * width, width), width)],
             dst_ref=cols.at[t, mine],
@@ -131,18 +140,51 @@
             device_id=device(x, y, zz, c), device_id_type=MESH,
         ).start()
 
-    for d in range(1, HALF):
-        for c in range(2):
-            send_columns(HALF - d, c)
-    send_columns(0, 1 - core)
+    def whole(k, d, c):
+        lo, n = {4: (0, tokens_in // 2), -4: (tokens_in // 2, tokens_in // 2)}.get(d, (0, tokens_in))
+        tt = (along(d) % HALF) * 2 + c
+        return pltpu.make_async_remote_copy(
+            src_ref=og.at[pl.ds(lo, n), pl.ds(pl.multiple_of(tt * width, width), width)],
+            dst_ref=cols.at[t, pl.ds(lo, n)],
+            send_sem=up_send.at[2 * k + c], recv_sem=col_recv,
+            device_id=device(x, y, along(d), c), device_id_type=MESH,
+        )
+
+    def whole_sibling():
+        tt = zl * 2 + 1 - core
+        return pltpu.make_async_remote_copy(
+            src_ref=og.at[:, pl.ds(pl.multiple_of(tt * width, width), width)],
+            dst_ref=cols.at[t],
+            send_sem=up_send.at[len(near)], recv_sem=col_recv,
+            device_id=device(x, y, z, 1 - core), device_id_type=MESH,
+        )
+
+    def send_up():
+        for k, d, c in near:
+            @pl.when(along(d) >= HALF)
+            def _():
+                whole(k, d, c).start()
+
+    @pl.when(lower)
+    def _():
+        own_part.start()
+        for d in range(1, HALF):
+            for c in range(2):
+                send_quarter(HALF - d, c)
+        send_quarter(0, 1 - core)
+
+    @pl.when(upper)
+    def _():
+        own_all.start()
+        send_up()
+        whole_sibling().start()
 
     wide[...] = jnp.zeros_like(wide)
     acc[...] = jnp.zeros_like(acc)
     pl.when(jnp.logical_not(early))(prepare)
 
-    own.wait()
     peers = cols.at[pl.ds(0, cols.shape[0] - 1), pl.ds(0, quarter)]
-    pltpu.make_async_copy(peers, peers, col_recv).wait()
+    blocks_in = cols.at[pl.ds(0, cols.shape[0] - 1)]
 
     def quarters(xx, lo, n):
         return cols.at[pl.ds(lo, n), pl.ds(pl.multiple_of(xx * quarter, quarter), quarter)]
@@ -161,17 +203,29 @@
         pltpu.make_async_copy(quarters(xx, lo, n), quarters(xx, lo, n), sem).wait()
 
     opposite = (x + 2) % NX
-    pass_on(x, 0, sources, right, 0)
-    pass_on(x, 0, sources, left, 1)
-    passed(left, 0, sources, x_recv.at[0])
-    pass_on(left, 0, half, right, 2)
-    passed(right, 0, sources, x_recv.at[1])
-    pass_on(right, half, half, left, 3)
+
+    @pl.when(lower)
+    def _():
+        own_part.wait()
+        pltpu.make_async_copy(peers, peers, col_recv).wait()
+        pass_on(x, 0, sources, right, 0)
+        pass_on(x, 0, sources, left, 1)
+        pl.semaphore_wait(upper_in, 2 * jnp.where(z < 4, 4 - z, z - 3))
+        send_up()
+        passed(left, 0, sources, x_recv.at[0])
+        pass_on(left, 0, half, right, 2)
+        passed(right, 0, sources, x_recv.at[1])
+        pass_on(right, half, half, left, 3)
+        passed(opposite, 0, half, x_recv.at[2])
+        passed(opposite, half, half, x_recv.at[3])
+
+    @pl.when(upper)
+    def _():
+        own_all.wait()
+        pltpu.make_async_copy(blocks_in, blocks_in, col_recv).wait()
 
     for copy in loads[2:]:
         copy.wait()
-    passed(opposite, 0, half, x_recv.at[2])
-    passed(opposite, half, half, x_recv.at[3])
     grad = jnp.dot(th[...], cols[...].reshape(tokens_all, width), preferred_element_type=jnp.float32)
     grad = grad * (1.0 / math.sqrt(tokens_all))
     new_first = 0.9 * fi[...] + 0.1 * grad
@@ -254,10 +308,6 @@
 
     for part in (1, 0):
         onward(0, 0, 0, part)
-
-    @pl.when(z != HALF)
-    def _():
-        pl.semaphore_wait(everyone, 1)
 
     zs = 4 * (1 - 2 * core)
     steps = (zs, -zs)
@@ -313,9 +363,21 @@
     final = pltpu.make_async_copy(dec, dec_hbm, out_sem.at[3])
     final.start()
 
-    pltpu.make_async_copy(peers, peers, col_send).wait()
-    for k, n in enumerate((sources, sources, half, half)):
-        passed(0, 0, n, x_send.at[k])
+    @pl.when(lower)
+    def _():
+        pltpu.make_async_copy(peers, peers, col_send).wait()
+        for k, n in enumerate((sources, sources, half, half)):
+            passed(0, 0, n, x_send.at[k])
+
+    @pl.when(upper)
+    def _():
+        whole_sibling().wait_send()
+
+    for k, d, c in near:
+        @pl.when(along(d) >= HALF)
+        def _():
+            whole(k, d, c).wait_send()
+
     for k in range(4):
         lo, n = PARTS[k % 2]
         pltpu.make_async_copy(relay.at[pl.ds(lo, n)], relay.at[pl.ds(lo, n)], z_send.at[k]).wait()
@@ -369,6 +431,7 @@
             pltpu.SemaphoreType.DMA((4,)),
             pltpu.SemaphoreType.DMA,
             pltpu.SemaphoreType.REGULAR,
+            pltpu.SemaphoreType.DMA((17,)),
             pltpu.SemaphoreType.DMA,
             pltpu.SemaphoreType.DMA((2 * NX * groups,)),
             pltpu.SemaphoreType.DMA((4,)),

time: 94.3 us -> 94.8 us (level)
  the two profiles are of different devices: /device:TPU:72 before, /device:TPU:256 now
where the time goes in v4:
time: 94.8 us; the launch traced here: 94.6 us
  Pallas kernels  94 us (99%)
    pallas_call x1, Pallas kernels, per_device(): pl.pallas_call(kernel, out_shape=(block, block, block, jax.ShapeDtypeStru...  91.8 us
    pallas_call x1, Pallas kernels, per_device(): pl.pallas_call(hand_on, out_shape=tuple((jax.ShapeDtypeStruct(a.shape, a....  2.16 us

profile of v4, /device:TPU:256, one launch (start us, length us, event | category | flops | bytes accessed | tf_op | source)
XLA Modules:
  0.0 94.6 jit_solution(2851286545861538908)
XLA Ops:
  0.6 91.8 %shard_map.93 = (f32[231,256]{1,0:T(8,128)}, f32[231,256]{1,0:T(8,128)}, f32[231,256]{1,0:T(8,128)}, bf16[256,256]{1,0:T(8,128)(2,1)}) custom-call(bf16[231,1024]{1,0:T(8,128)(2,1)} %bitcast.3, bf16[64,4096]{1,0:T(8,128)(2,1)} %og_hbm.1, f32[231,256]{1,0:T(8,128)} %ma_hbm.1, f32[231,256]{1,0:T(8,128)} %fi_hbm.1, f32[231,256]{1,0:T(8,128)} %se_hbm.1, ...), custom_call_target="tpu_custom_call" | custom-call | tf_op jit(solution)/shard_map/pallas_call | solution.py:404
  92.5 2.2 %shard_map.94 = (f32[231,256]{1,0:T(8,128)}, f32[231,256]{1,0:T(8,128)}, f32[231,256]{1,0:T(8,128)}, bf16[256,256]{1,0:T(8,128)(2,1)}) custom-call(f32[231,256]{1,0:T(8,128)} %get-tuple-element.8.refs_0_, f32[231,256]{1,0:T(8,128)} %get-tuple-element.9.refs_1_, f32[231,256]{1,0:T(8,128)} %get-tuple-element.10.refs_2_, bf16[256,256]{1,0:T(8,128)(2,1)} %get-tuple-element.11.refs_3_), custom_call_target="tpu_custom_call" | custom-call | tf_op jit(solution)/shard_map/pallas_call | solution.py:444

commit v5 on v2

--- a/solution.py
+++ b/solution.py
@@ -11,7 +11,7 @@
 NX, NY, NZ = 4, 8, 16
 HALF = NZ // 2
 SLOT = 256
-SENT = 240
+SENT = 232
 CUT = 96
 PARTS = ((0, CUT), (CUT, SENT - CUT))
 RELAY_AFTER = 1
@@ -267,7 +267,7 @@
     for k in range(4):
         lo, n = PARTS[k % 2]
         pltpu.make_async_copy(relay.at[pl.ds(lo, n)], relay.at[pl.ds(lo, n)], z_send.at[k]).wait()
-    window = w.at[pl.ds(0, 2 * NY - 1), pl.ds(0, 2 * (NX * NY - 1) * SENT // (2 * NY - 1))]
+    window = dh.at[pl.ds(0, 2 * (NX * NY - 1) * SENT)]
     pltpu.make_async_copy(window, window, w_send).wait()
     for copy in outs:
         copy.wait()

time: 89.3 us -> 88.3 us (0.989)
  the two profiles are of different devices: /device:TPU:8 before, /device:TPU:14 now
where the time goes in v5:
time: 88.3 us; the launch traced here: 88.1 us
  Pallas kernels  87.5 us (99%)
    pallas_call x1, Pallas kernels, per_device(): pl.pallas_call(kernel, out_shape=(block, block, block, jax.ShapeDtypeStru...  85.3 us
    pallas_call x1, Pallas kernels, per_device(): pl.pallas_call(hand_on, out_shape=tuple((jax.ShapeDtypeStruct(a.shape, a....  2.16 us

profile of v5, /device:TPU:14, one launch (start us, length us, event | category | flops | bytes accessed | tf_op | source)
XLA Modules:
  0.0 88.1 jit_solution(3095417464153869997)
XLA Ops:
  0.6 85.3 %shard_map.93 = (f32[231,256]{1,0:T(8,128)}, f32[231,256]{1,0:T(8,128)}, f32[231,256]{1,0:T(8,128)}, bf16[256,256]{1,0:T(8,128)(2,1)}) custom-call(bf16[231,1024]{1,0:T(8,128)(2,1)} %bitcast.3, bf16[64,4096]{1,0:T(8,128)(2,1)} %og_hbm.1, f32[231,256]{1,0:T(8,128)} %ma_hbm.1, f32[231,256]{1,0:T(8,128)} %fi_hbm.1, f32[231,256]{1,0:T(8,128)} %se_hbm.1, ...), custom_call_target="tpu_custom_call" | custom-call | tf_op jit(solution)/shard_map/pallas_call | solution.py:290
  85.9 2.2 %shard_map.94 = (f32[231,256]{1,0:T(8,128)}, f32[231,256]{1,0:T(8,128)}, f32[231,256]{1,0:T(8,128)}, bf16[256,256]{1,0:T(8,128)(2,1)}) custom-call(f32[231,256]{1,0:T(8,128)} %get-tuple-element.8.refs_0_, f32[231,256]{1,0:T(8,128)} %get-tuple-element.9.refs_1_, f32[231,256]{1,0:T(8,128)} %get-tuple-element.10.refs_2_, bf16[256,256]{1,0:T(8,128)(2,1)} %get-tuple-element.11.refs_3_), custom_call_target="tpu_custom_call" | custom-call | tf_op jit(solution)/shard_map/pallas_call | solution.py:326
